TPU v7x, 256 devices: a whole 4x4x8 slice. The times are simulated.
256 devices in a mesh: tc: 128 (over z, x, y), pr: 2 (over core).
Axes of the slice: x: 4, y: 4, z: 8, core: 2. Of those that a mesh axis runs over, the one named last changes fastest.
Arguments:
- pivot_rhs: float32 [128, 1536, 64], P('tc', None, 'pr'), may hold values from -6 to 6
- pivot_inverse: bfloat16 [128, 1536, 1536], P('tc'), as said below
- pivot_owner: int32 [3], replicated, may hold values from 0 to 127, as said below
- coupling_left: bfloat16 [128, 2, 1536, 200], P('tc'), may hold values from -0.15625 to 0.15625
- coupling_right: bfloat16 [128, 2, 1536, 200], P('tc'), may hold values from -0.4375 to 0.4375
- coupling_ranks: int32 [128, 2], P('tc'), may hold values from 100 to 200, as said below
- future_left: bfloat16 [256, 3, 200, 1536], P('tc', None, None, 'pr'), may hold values from -0.15625 to 0.15625
- future_right: bfloat16 [256, 3, 200, 1536], P('tc', None, None, 'pr'), may hold values from -0.4375 to 0.4375
- future_ranks: int32 [256, 3], P('tc'), may hold values from 100 to 200, as said below
- future_rhs: float32 [256, 64, 1536], P('tc', None, 'pr'), may hold values from -6 to 6
Outputs:
- solved: bfloat16 [3, 1536, 64], P(None, None, 'pr')
- future_out: float32 [256, 64, 1536], P('tc', None, 'pr')
Inputs may be any that keep to these rules, and one draw needn't show every extreme that they name: `pivot_owner`: the 3 entries are distinct; entry p names the slot, and so the index of tc, that holds pivot p's tiles. `coupling_ranks`: entry [s, j] is the rank of the tile from the pivot in slot s to the pivot j + 1 places later. In every draw a tile that the window uses has rank exactly 200. `future_ranks`: in every draw one of these tiles has rank exactly 200. `pivot_inverse`: each tile is lower triangular.
All inputs are finite; a program needn't handle non-finite values.
Results may differ from a plain program's by a relative error of at most 0.007.
Values may be sent and summed in bfloat16 or wider, within the bound.
A program may use at most 64 MiB of HBM per device.

v0:
```python
import jax
import jax.numpy as jnp
from jax import lax
from jax.sharding import Mesh
from jax.sharding import PartitionSpec as P

TC = ("tc_0", "tc_1", "tc_2")


def padded_to(lines, count):
    spare = -lines.shape[0] % count
    if not spare:
        return lines
    return jnp.concatenate([lines, jnp.zeros((spare, *lines.shape[1:]), lines.dtype)])


def sent_to_all(shard, axis):
    count = lax.axis_size(axis)
    return lax.all_to_all(
        jnp.broadcast_to(shard[None], (count, *shard.shape)), axis, 0, 0, tiled=True
    )


def in_order(pieces, dim):
    pieces = jnp.moveaxis(pieces, 0, dim)
    shape = pieces.shape
    return pieces.reshape(*shape[:dim], shape[dim] * shape[dim + 1], *shape[dim + 2 :])


def gathered_by_axis(shard, axes, dim):
    far, near = axes
    pieces = sent_to_all(sent_to_all(shard, far), near)
    return in_order(pieces.swapaxes(0, 1).reshape(-1, *shard.shape), dim)


def in_blocks(shard, dim, count):
    shape = shard.shape
    pieces = shard.reshape(*shape[:dim], count, shape[dim] // count, *shape[dim + 1 :])
    return jnp.moveaxis(pieces, dim, 0)


def sum_at_owner(shard, axis, dim):
    pieces = in_blocks(shard, dim, lax.axis_size(axis))
    arrived = lax.all_to_all(pieces, axis, split_axis=0, concat_axis=0, tiled=True)
    return arrived.sum(axis=0)


def summed_rows(shard, axes, dim):
    far, near = axes
    own = sum_at_owner(in_blocks(shard, dim, lax.axis_size(far)), near, dim + 1)
    return jnp.sum(lax.all_to_all(own, far, 0, 0, tiled=True), axis=0)


def nested_sum(shard, axes):
    lines = shard.reshape(-1, shard.shape[-1])
    padded = padded_to(lines, lax.axis_size(axes[0]) * lax.axis_size(axes[1]))
    whole = gathered_by_axis(summed_rows(padded, axes, 0), axes, 0)
    return lax.slice_in_dim(whole, 0, len(lines)).reshape(shard.shape)


def over_copies(shard, axis):
    return sent_to_all(shard, axis).sum(axis=0)


def apply_weights(products, right_part, ranks_part):
    rank_ids = lax.broadcasted_iota(jnp.int32, products.shape, 3)
    weights = jnp.where(rank_ids < ranks_part[:, :, None, None], products, 0.0).astype(jnp.bfloat16)
    return jnp.einsum("fsqr,fsrb->fqb", weights, right_part, preferred_element_type=jnp.float32)


def local(
    pivot_rhs,
    pivot_inverse,
    pivot_owner,
    coupling_left,
    coupling_right,
    coupling_ranks,
    future_left,
    future_right,
    future_ranks,
    future_rhs,
):
    tile_count = pivot_owner.shape[0]
    rank_width = coupling_left.shape[3]
    device_index = lax.axis_index(TC)
    owned_flags = pivot_owner == device_index
    holds_pivot = jnp.any(owned_flags)
    own_pivot = jnp.sum(jnp.where(owned_flags, jnp.arange(tile_count, dtype=jnp.int32), 0))
    pending = pivot_rhs[0]
    inverse_tile = pivot_inverse[0]
    rank_ids = lax.broadcasted_iota(jnp.int32, (rank_width, 1), 0)
    solved = [None] * tile_count
    future_acc = future_rhs
    for current in reversed(range(tile_count)):
        pivot_in = pending.astype(jnp.bfloat16)
        local_solution = lax.dot_general(
            inverse_tile, pivot_in, (((0,), (0,)), ((), ())), preferred_element_type=jnp.float32
        ).astype(jnp.bfloat16)
        is_root = device_index == pivot_owner[current]
        masked_block = jnp.where(is_root, local_solution.astype(jnp.float32), 0.0)
        solved_block = nested_sum(masked_block, (("tc_0", "tc_1"), "tc_2")).astype(jnp.bfloat16)
        solved[current] = solved_block
        if current > 0:
            distance = current - own_pivot - 1
            active = jnp.logical_and(holds_pivot, distance >= 0)
            slot_entry = jnp.clip(distance, 0, tile_count - 2)
            left_tile = lax.dynamic_index_in_dim(coupling_left[0], slot_entry, 0, keepdims=False)
            right_tile = lax.dynamic_index_in_dim(coupling_right[0], slot_entry, 0, keepdims=False)
            rank_limit = lax.dynamic_index_in_dim(coupling_ranks[0], slot_entry, 0, keepdims=False)
            factor = lax.dot_general(
                left_tile,
                solved_block,
                (((0,), (0,)), ((), ())),
                preferred_element_type=jnp.float32,
            )
            factor = jnp.where(rank_ids < rank_limit, factor, 0.0).astype(jnp.bfloat16)
            change = jnp.dot(right_tile, factor, preferred_element_type=jnp.float32)
            pending = pending - jnp.where(active, change, 0.0)
    stacked = jnp.stack(solved)
    columns = lax.all_to_all(stacked, "pr", split_axis=1, concat_axis=2, tiled=True)
    products = jnp.einsum(
        "sbq,fsrb->fsqr", columns, future_left, preferred_element_type=jnp.float32
    )
    products = over_copies(products, "pr")
    future_acc = future_acc - apply_weights(products, future_right, future_ranks)
    return (stacked, future_acc)


def solution(mesh):
    finer = Mesh(mesh.devices.reshape(8, 4, 4, mesh.shape["pr"]), ("tc_0", "tc_1", "tc_2", "pr"))
    in_specs = (
        P(TC, None, "pr"),
        P(TC, None, None),
        P(),
        P(TC, None, None, None),
        P(TC, None, None, None),
        P(TC, None),
        P(TC, None, None, "pr"),
        P(TC, None, None, "pr"),
        P(TC, None),
        P(TC, None, "pr"),
    )
    out_specs = (P(None, None, "pr"), P(TC, None, "pr"))
    return jax.shard_map(local, mesh=finer, in_specs=in_specs, out_specs=out_specs, check_vma=False)
```

profile of v0, /device:TPU:1, one launch (start us, length us, event | category | flops | bytes accessed | tf_op | source)
XLA Modules:
  0.0 229.7 jit_solution(5553572700771871744)
XLA Ops:
  2.7 3.3 %fusion.15 = f32[1536,32]{0,1:T(8,128)S(1)} fusion(bf16[1,1536,1536]{2,1,0:T(8,128)(2,1)} %param.11, f32[1,1536,32]{1,2,0:T(8,128)} %param.10, pred[]{:T(512)S(6)} %eq.18), kind=kOutput, calls=%fused_computation.13 | convolution fusion | flops 151191552 | bytes 5111809 | tf_op jit(solution)/shard_map/dot_general | solution.py:96
  11.3 10.0 %all_to_all.83 = f32[4,1,12288]{2,1,0:T(1,128)S(1)} all-to-all(f32[4,1,12288]{2,1,0:T(1,128)S(1)} %reshape.72), channel_id=1, replica_groups=mesh['tc_0'=8,'tc_1'=4,'tc_2'=4,'pr'=2] {'tc_2'}, dimensions={0} | all-to-all | bytes 393216 | tf_op jit(solution)/shard_map/all_to_all | solution.py:44
  24.1 11.0 %all-to-all-start.1 = ((f32[32,1,384]{2,1,0:T(1,128)}), f32[32,1,384]{2,1,0:T(1,128)S(1)}, u32[]{:S(2)}, u32[]{:S(2)}) async-start(f32[32,1,384]{2,1,0:T(1,128)} %reshape.74), calls=%async_computation.1 | async-start | bytes 98304 | tf_op jit(solution)/shard_map/all_to_all | solution.py:51
  35.9 8.0 %all-to-all-done.1 = f32[32,1,384]{2,1,0:T(1,128)S(1)} async-done(((f32[32,1,384]{2,1,0:T(1,128)}), f32[32,1,384]{2,1,0:T(1,128)S(1)}, u32[]{:S(2)}, u32[]{:S(2)}) %all-to-all-start.1) | async-done | bytes 49184 | tf_op jit(solution)/shard_map/all_to_all | solution.py:51
  45.5 3.9 %all-to-all-start.2 = ((bf16[32,2,192]{2,1,0:T(2,128)(2,1)}), bf16[32,2,192]{2,1,0:T(2,128)(2,1)S(1)}, u32[]{:S(2)}, u32[]{:S(2)}) async-start(bf16[32,2,192]{2,1,0:T(2,128)(2,1)} %reshape.76), calls=%async_computation.2 | async-start | bytes 65536 | tf_op jit(solution)/shard_map/all_to_all | solution.py:19
  53.2 4.8 %all-to-all-done.2 = bf16[32,2,192]{2,1,0:T(2,128)(2,1)S(1)} async-done(((bf16[32,2,192]{2,1,0:T(2,128)(2,1)}), bf16[32,2,192]{2,1,0:T(2,128)(2,1)S(1)}, u32[]{:S(2)}, u32[]{:S(2)}) %all-to-all-start.2) | async-done | bytes 24608 | tf_op jit(solution)/shard_map/all_to_all | solution.py:19
  59.3 3.3 %all-to-all-start.3 = ((bf16[4,2,6144]{2,1,0:T(2,128)(2,1)}), bf16[4,2,6144]{2,1,0:T(2,128)(2,1)S(1)}, u32[]{:S(2)}, u32[]{:S(2)}) async-start(bf16[4,2,6144]{2,1,0:T(2,128)(2,1)} %reshape.78), calls=%async_computation.3 | async-start | bytes 196608 | tf_op jit(solution)/shard_map/all_to_all | solution.py:19
  63.3 3.9 %all-to-all-done.3 = bf16[4,2,6144]{2,1,0:T(2,128)(2,1)S(1)} async-done(((bf16[4,2,6144]{2,1,0:T(2,128)(2,1)}), bf16[4,2,6144]{2,1,0:T(2,128)(2,1)S(1)}, u32[]{:S(2)}, u32[]{:S(2)}) %all-to-all-start.3) | async-done | bytes 98336 | tf_op jit(solution)/shard_map/all_to_all | solution.py:19
  69.8 3.3 %fusion.27 = f32[1536,32]{0,1:T(8,128)S(1)} fusion(bf16[1,1536,1536]{2,1,0:T(8,128)(2,1)} %param.11, f32[1536,32]{0,1:T(8,128)S(1)} %fusion.6, pred[]{:T(512)S(6)} %eq.19), kind=kOutput, calls=%fused_computation.17 | convolution fusion | flops 151191552 | bytes 5111809 | tf_op jit(solution)/shard_map/dot_general | solution.py:96
  78.3 7.5 %all_to_all.84 = f32[4,1,12288]{2,1,0:T(1,128)S(1)} all-to-all(f32[4,1,12288]{2,1,0:T(1,128)S(1)} %reshape.80), channel_id=1, replica_groups=mesh['tc_0'=8,'tc_1'=4,'tc_2'=4,'pr'=2] {'tc_2'}, dimensions={0} | all-to-all | bytes 393216 | tf_op jit(solution)/shard_map/all_to_all | solution.py:44
  87.6 12.9 %all_to_all.85 = f32[32,1,384]{2,1,0:T(1,128)S(1)} all-to-all(f32[32,1,384]{2,1,0:T(1,128)S(1)} %reshape.82), channel_id=1, replica_groups=mesh['tc_0'=8,'tc_1'=4,'tc_2'=4,'pr'=2] {'tc_0','tc_1'}, dimensions={0} | all-to-all | bytes 98304 | tf_op jit(solution)/shard_map/all_to_all | solution.py:51
  102.2 3.9 %all-to-all-start.6 = ((bf16[32,2,192]{2,1,0:T(2,128)(2,1)}), bf16[32,2,192]{2,1,0:T(2,128)(2,1)S(1)}, u32[]{:S(2)}, u32[]{:S(2)}) async-start(bf16[32,2,192]{2,1,0:T(2,128)(2,1)} %reshape.84), calls=%async_computation.6 | async-start | bytes 65536 | tf_op jit(solution)/shard_map/all_to_all | solution.py:19
  107.2 7.4 %all-to-all-done.6 = bf16[32,2,192]{2,1,0:T(2,128)(2,1)S(1)} async-done(((bf16[32,2,192]{2,1,0:T(2,128)(2,1)}), bf16[32,2,192]{2,1,0:T(2,128)(2,1)S(1)}, u32[]{:S(2)}, u32[]{:S(2)}) %all-to-all-start.6) | async-done | bytes 24608 | tf_op jit(solution)/shard_map/all_to_all | solution.py:19
  115.9 3.5 %all-to-all-start.7 = ((bf16[4,2,6144]{2,1,0:T(2,128)(2,1)}), bf16[4,2,6144]{2,1,0:T(2,128)(2,1)S(1)}, u32[]{:S(2)}, u32[]{:S(2)}) async-start(bf16[4,2,6144]{2,1,0:T(2,128)(2,1)} %reshape.86), calls=%async_computation.7 | async-start | bytes 196608 | tf_op jit(solution)/shard_map/all_to_all | solution.py:19
  120.1 3.7 %all-to-all-done.7 = bf16[4,2,6144]{2,1,0:T(2,128)(2,1)S(1)} async-done(((bf16[4,2,6144]{2,1,0:T(2,128)(2,1)}), bf16[4,2,6144]{2,1,0:T(2,128)(2,1)S(1)}, u32[]{:S(2)}, u32[]{:S(2)}) %all-to-all-start.7) | async-done | bytes 98336 | tf_op jit(solution)/shard_map/all_to_all | solution.py:19
  127.0 3.3 %fusion.39 = f32[1536,32]{0,1:T(8,128)S(1)} fusion(bf16[1536,32]{0,1:T(8,128)(2,1)} %fusion.8, bf16[1,1536,1536]{2,1,0:T(8,128)(2,1)} %param.11, pred[]{:T(512)S(6)} %eq.15), kind=kOutput, calls=%fused_computation.21 | convolution fusion | flops 151142400 | bytes 5013505 | tf_op jit(solution)/shard_map/dot_general | solution.py:96
  137.8 7.5 %all_to_all.86 = f32[4,1,12288]{2,1,0:T(1,128)S(1)} all-to-all(f32[4,1,12288]{2,1,0:T(1,128)S(1)} %reshape.88), channel_id=1, replica_groups=mesh['tc_0'=8,'tc_1'=4,'tc_2'=4,'pr'=2] {'tc_2'}, dimensions={0} | all-to-all | bytes 393216 | tf_op jit(solution)/shard_map/all_to_all | solution.py:44
  149.2 11.7 %all_to_all.87 = f32[32,1,384]{2,1,0:T(1,128)S(1)} all-to-all(f32[32,1,384]{2,1,0:T(1,128)S(1)} %reshape.90), channel_id=1, replica_groups=mesh['tc_0'=8,'tc_1'=4,'tc_2'=4,'pr'=2] {'tc_0','tc_1'}, dimensions={0} | all-to-all | bytes 98304 | tf_op jit(solution)/shard_map/all_to_all | solution.py:51
  161.9 11.6 %all_to_all.88 = bf16[32,2,192]{2,1,0:T(2,128)(2,1)S(1)} all-to-all(bf16[32,2,192]{2,1,0:T(2,128)(2,1)S(1)} %reshape.92), channel_id=1, replica_groups=mesh['tc_0'=8,'tc_1'=4,'tc_2'=4,'pr'=2] {'tc_0','tc_1'}, dimensions={0} | all-to-all | bytes 49152 | tf_op jit(solution)/shard_map/all_to_all | solution.py:19
  174.8 3.3 %all-to-all-start.11 = ((bf16[4,2,6144]{2,1,0:T(2,128)(2,1)}), bf16[4,2,6144]{2,1,0:T(2,128)(2,1)S(1)}, u32[]{:S(2)}, u32[]{:S(2)}) async-start(bf16[4,2,6144]{2,1,0:T(2,128)(2,1)} %reshape.94), calls=%async_computation.11 | async-start | bytes 196608 | tf_op jit(solution)/shard_map/all_to_all | solution.py:19
  179.2 3.8 %all-to-all-done.11 = bf16[4,2,6144]{2,1,0:T(2,128)(2,1)S(1)} async-done(((bf16[4,2,6144]{2,1,0:T(2,128)(2,1)}), bf16[4,2,6144]{2,1,0:T(2,128)(2,1)S(1)}, u32[]{:S(2)}, u32[]{:S(2)}) %all-to-all-start.11) | async-done | bytes 98336 | tf_op jit(solution)/shard_map/all_to_all | solution.py:19
  187.6 8.2 %copy.136 = bf16[3,1536,32]{2,0,1:T(4,128)(2,1)} copy(bf16[3,1536,32]{2,1,0:T(8,128)(2,1)S(1)} %constant_dynamic-update-slice_fusion) | data formatting | bytes 589824 | tf_op jit(solution)/shard_map/stack | solution.py:119
  198.1 18.6 %all_to_all.89 = bf16[2,2,36864]{2,1,0:T(2,128)(2,1)} all-to-all(bf16[2,2,36864]{2,1,0:T(2,128)(2,1)S(1)} %reshape.96), channel_id=1, replica_groups=mesh['tc_0'=8,'tc_1'=4,'tc_2'=4,'pr'=2] {'pr'}, dimensions={0} | all-to-all | bytes 589824 | tf_op jit(solution)/shard_map/all_to_all | solution.py:120
  223.8 4.5 %all_to_all.90 = f32[2,2,3,64,200]{4,3,2,1,0:T(8,128)S(1)} all-to-all(f32[2,2,3,64,200]{4,3,2,1,0:T(8,128)S(1)} %broadcast_in_dim.91), channel_id=1, replica_groups=mesh['tc_0'=8,'tc_1'=4,'tc_2'=4,'pr'=2] {'pr'}, dimensions={0} | all-to-all | bytes 1228800 | tf_op jit(solution)/shard_map/all_to_all | solution.py:19
  (106 shorter events, 61.0 us)
Async XLA Ops:
  0.6 227.7 %copy-start = (bf16[2,3,200,768]{3,2,1,0:T(8,128)(2,1)S(1)}, bf16[2,3,200,768]{3,2,1,0:T(8,128)(2,1)}, u32[]{:S(2)}) copy-start(bf16[2,3,200,768]{3,2,1,0:T(8,128)(2,1)} %param.17) | copy-start | bytes 5529604
  21.8 13.4 %copy-start.5 = (s32[3]{0:T(128)S(1)}, s32[3]{0:T(128)}, u32[]{:S(2)}) copy-start(s32[3]{0:T(128)} %param.12) | copy-start | bytes 40
  23.2 29.4 %copy-start.7 = (s32[1,2]{1,0:T(1,128)S(1)}, s32[1,2]{1,0:T(1,128)}, u32[]{:S(2)}) copy-start(s32[1,2]{1,0:T(1,128)} %param.15) | copy-start | bytes 28
  24.1 19.8 %all-to-all-start.1 = ((f32[32,1,384]{2,1,0:T(1,128)}), f32[32,1,384]{2,1,0:T(1,128)S(1)}, u32[]{:S(2)}, u32[]{:S(2)}) async-start(f32[32,1,384]{2,1,0:T(1,128)} %reshape.74), calls=%async_computation.1 | async-start | bytes 98304 | tf_op jit(solution)/shard_map/all_to_all | solution.py:51
  45.5 12.5 %all-to-all-start.2 = ((bf16[32,2,192]{2,1,0:T(2,128)(2,1)}), bf16[32,2,192]{2,1,0:T(2,128)(2,1)S(1)}, u32[]{:S(2)}, u32[]{:S(2)}) async-start(bf16[32,2,192]{2,1,0:T(2,128)(2,1)} %reshape.76), calls=%async_computation.2 | async-start | bytes 65536 | tf_op jit(solution)/shard_map/all_to_all | solution.py:19
  59.3 7.9 %all-to-all-start.3 = ((bf16[4,2,6144]{2,1,0:T(2,128)(2,1)}), bf16[4,2,6144]{2,1,0:T(2,128)(2,1)S(1)}, u32[]{:S(2)}, u32[]{:S(2)}) async-start(bf16[4,2,6144]{2,1,0:T(2,128)(2,1)} %reshape.78), calls=%async_computation.3 | async-start | bytes 196608 | tf_op jit(solution)/shard_map/all_to_all | solution.py:19
  62.6 5.2 %copy-start.3 = (f32[1,1536,32]{1,2,0:T(8,128)S(1)}, f32[1,1536,32]{1,2,0:T(8,128)}, u32[]{:S(2)}) copy-start(f32[1,1536,32]{1,2,0:T(8,128)} %param.10) | copy-start | bytes 589828
  69.8 3.3 %copy-start.1 = (f32[1536,32]{0,1:T(8,128)}, f32[1536,32]{0,1:T(8,128)S(1)}, u32[]{:S(2)}) copy-start(f32[1536,32]{0,1:T(8,128)S(1)} %fusion.6) | copy-start | bytes 589828
  102.2 12.5 %all-to-all-start.6 = ((bf16[32,2,192]{2,1,0:T(2,128)(2,1)}), bf16[32,2,192]{2,1,0:T(2,128)(2,1)S(1)}, u32[]{:S(2)}, u32[]{:S(2)}) async-start(bf16[32,2,192]{2,1,0:T(2,128)(2,1)} %reshape.84), calls=%async_computation.6 | async-start | bytes 65536 | tf_op jit(solution)/shard_map/all_to_all | solution.py:19
  115.9 7.9 %all-to-all-start.7 = ((bf16[4,2,6144]{2,1,0:T(2,128)(2,1)}), bf16[4,2,6144]{2,1,0:T(2,128)(2,1)S(1)}, u32[]{:S(2)}, u32[]{:S(2)}) async-start(bf16[4,2,6144]{2,1,0:T(2,128)(2,1)} %reshape.86), calls=%async_computation.7 | async-start | bytes 196608 | tf_op jit(solution)/shard_map/all_to_all | solution.py:19
  119.4 5.0 %copy-start.2 = (f32[1536,32]{0,1:T(8,128)S(1)}, f32[1536,32]{0,1:T(8,128)}, u32[]{:S(2)}) copy-start(f32[1536,32]{0,1:T(8,128)} %copy-done.1) | copy-start | bytes 589828
  174.8 8.2 %all-to-all-start.11 = ((bf16[4,2,6144]{2,1,0:T(2,128)(2,1)}), bf16[4,2,6144]{2,1,0:T(2,128)(2,1)S(1)}, u32[]{:S(2)}, u32[]{:S(2)}) async-start(bf16[4,2,6144]{2,1,0:T(2,128)(2,1)} %reshape.94), calls=%async_computation.11 | async-start | bytes 196608 | tf_op jit(solution)/shard_map/all_to_all | solution.py:19
  223.8 4.6 %copy-start.4 = (f32[2,64,768]{2,1,0:T(8,128)S(1)}, f32[2,64,768]{2,1,0:T(8,128)}, u32[]{:S(2)}) copy-start(f32[2,64,768]{2,1,0:T(8,128)} %param.19) | copy-start | bytes 1179652
  223.8 4.6 %copy-start.6 = (s32[2,3]{1,0:T(2,128)S(1)}, s32[2,3]{1,0:T(2,128)}, u32[]{:S(2)}) copy-start(s32[2,3]{1,0:T(2,128)} %param.18) | copy-start | bytes 76
where the time goes:
time: 231 us; the launch traced here: 230 us
  blocking collectives  84.4 us (37%)
  local copies, waits for them, and re-layouts  51.5 us (22%)
  waiting for transfers between devices  31.7 us (14%)
  starting transfers between devices  28.8 us (12%)
  matrix products  17.9 us (8%)
  other arithmetic  9.7 us (4%)
  between operations  5.64 us (2%)
    all_to_all x3, blocking collectives, sum_at_owner(): lax.all_to_all(pieces, axis, split_axis=0, concat_axis=0, tiled=True)  25.1 us
    all_to_all x2, blocking collectives, summed_rows(): return jnp.sum(lax.all_to_all(own, far, 0, 0, tiled=True), axis=0)  24.7 us
    all_to_all x5, waiting for transfers between devices, sent_to_all(): lax.all_to_all(jnp.broadcast_to(shard[None], (count, *shard.shape)), axis...  23.7 us
    unnamed x48, local copies, waits for them, and re-layouts  20.9 us
    all_to_all x1, blocking collectives, local(): lax.all_to_all(stacked, 'pr', split_axis=1, concat_axis=2, tiled=True)  18.6 us
    all_to_all x5, starting transfers between devices, sent_to_all(): lax.all_to_all(jnp.broadcast_to(shard[None], (count, *shard.shape)), axis...  17.8 us
    all_to_all x2, blocking collectives, sent_to_all(): lax.all_to_all(jnp.broadcast_to(shard[None], (count, *shard.shape)), axis...  16.1 us
    all_to_all x1, starting transfers between devices, summed_rows(): return jnp.sum(lax.all_to_all(own, far, 0, 0, tiled=True), axis=0)  11 us
  transfers between devices with their start and end apart: 6, of which 6 were waited for; matrix products, arithmetic and copies ran while one was open for 2% of the time, Pallas kernels for 0%

commit v1 on v0

--- a/solution.py
+++ b/solution.py
@@ -117,7 +117,10 @@
             change = jnp.dot(right_tile, factor, preferred_element_type=jnp.float32)
             pending = pending - jnp.where(active, change, 0.0)
     stacked = jnp.stack(solved)
-    columns = lax.all_to_all(stacked, "pr", split_axis=1, concat_axis=2, tiled=True)
+    columns = jnp.concatenate(
+        lax.all_to_all(jnp.stack(jnp.split(stacked, lax.axis_size("pr"), axis=1)), "pr", 0, 0),
+        axis=2,
+    )
     products = jnp.einsum(
         "sbq,fsrb->fsqr", columns, future_left, preferred_element_type=jnp.float32
     )

time: 231 us -> 210 us (0.909)
  local copies, waits for them, and re-layouts: 51.5 us -> 32 us
    another operation x2 -> x1, local copies, waits for them, and re-layouts: 8.25 us -> 0.02 us  [local(): jnp.stack(jnp.split(stacked, lax.axis_size('pr'), axis=1))]
    unnamed x48 -> x47, local copies, waits for them, and re-layouts: 20.9 us -> 13.5 us
    all_to_all x2 -> x1, local copies, waits for them, and re-layouts: 2.83 us -> 0.02 us  [local(): lax.all_to_all(jnp.stack(jnp.split(stacked, lax.axis_size('pr'), axis=1))...]
where the time goes in v1:
time: 210 us; the launch traced here: 209 us
  blocking collectives  83.8 us (40%)
  waiting for transfers between devices  32.2 us (15%)
  local copies, waits for them, and re-layouts  32 us (15%)
  starting transfers between devices  28.8 us (14%)
  matrix products  16.4 us (8%)
  other arithmetic  9.68 us (5%)
  between operations  5.68 us (3%)
    all_to_all x3, blocking collectives, sum_at_owner(): lax.all_to_all(pieces, axis, split_axis=0, concat_axis=0, tiled=True)  25.1 us
    all_to_all x2, blocking collectives, summed_rows(): return jnp.sum(lax.all_to_all(own, far, 0, 0, tiled=True), axis=0)  24.7 us
    all_to_all x5, waiting for transfers between devices, sent_to_all(): lax.all_to_all(jnp.broadcast_to(shard[None], (count, *shard.shape)), axis...  24.2 us
    all_to_all x1, blocking collectives, local(): lax.all_to_all(jnp.stack(jnp.split(stacked, lax.axis_size('pr'), axis=1))...  18 us
    all_to_all x5, starting transfers between devices, sent_to_all(): lax.all_to_all(jnp.broadcast_to(shard[None], (count, *shard.shape)), axis...  17.8 us
    all_to_all x2, blocking collectives, sent_to_all(): lax.all_to_all(jnp.broadcast_to(shard[None], (count, *shard.shape)), axis...  16.1 us
    unnamed x47, local copies, waits for them, and re-layouts  13.5 us
    all_to_all x1, starting transfers between devices, summed_rows(): return jnp.sum(lax.all_to_all(own, far, 0, 0, tiled=True), axis=0)  11 us
  transfers between devices with their start and end apart: 6, of which 6 were waited for; matrix products, arithmetic and copies ran while one was open for 2% of the time, Pallas kernels for 0%

profile of v1, /device:TPU:1, one launch (start us, length us, event | category | flops | bytes accessed | tf_op | source)
XLA Modules:
  0.0 208.7 jit_solution(14747441125403757951)
XLA Ops:
  2.7 3.3 %fusion.15 = f32[1536,32]{0,1:T(8,128)S(1)} fusion(bf16[1,1536,1536]{2,1,0:T(8,128)(2,1)} %param.11, f32[1,1536,32]{1,2,0:T(8,128)} %param.10, pred[]{:T(512)S(6)} %eq.18), kind=kOutput, calls=%fused_computation.13 | convolution fusion | flops 151191552 | bytes 5111809 | tf_op jit(solution)/shard_map/dot_general | solution.py:96
  11.3 10.0 %all_to_all.70 = f32[4,1,12288]{2,1,0:T(1,128)S(1)} all-to-all(f32[4,1,12288]{2,1,0:T(1,128)S(1)} %reshape.80), channel_id=1, replica_groups=mesh['tc_0'=8,'tc_1'=4,'tc_2'=4,'pr'=2] {'tc_2'}, dimensions={0} | all-to-all | bytes 393216 | tf_op jit(solution)/shard_map/all_to_all | solution.py:44
  24.1 11.0 %all-to-all-start.1 = ((f32[32,1,384]{2,1,0:T(1,128)}), f32[32,1,384]{2,1,0:T(1,128)S(1)}, u32[]{:S(2)}, u32[]{:S(2)}) async-start(f32[32,1,384]{2,1,0:T(1,128)} %reshape.82), calls=%async_computation.1 | async-start | bytes 98304 | tf_op jit(solution)/shard_map/all_to_all | solution.py:51
  35.9 8.0 %all-to-all-done.1 = f32[32,1,384]{2,1,0:T(1,128)S(1)} async-done(((f32[32,1,384]{2,1,0:T(1,128)}), f32[32,1,384]{2,1,0:T(1,128)S(1)}, u32[]{:S(2)}, u32[]{:S(2)}) %all-to-all-start.1) | async-done | bytes 49184 | tf_op jit(solution)/shard_map/all_to_all | solution.py:51
  45.5 3.9 %all-to-all-start.2 = ((bf16[32,2,192]{2,1,0:T(2,128)(2,1)}), bf16[32,2,192]{2,1,0:T(2,128)(2,1)S(1)}, u32[]{:S(2)}, u32[]{:S(2)}) async-start(bf16[32,2,192]{2,1,0:T(2,128)(2,1)} %reshape.84), calls=%async_computation.2 | async-start | bytes 65536 | tf_op jit(solution)/shard_map/all_to_all | solution.py:19
  53.2 4.8 %all-to-all-done.2 = bf16[32,2,192]{2,1,0:T(2,128)(2,1)S(1)} async-done(((bf16[32,2,192]{2,1,0:T(2,128)(2,1)}), bf16[32,2,192]{2,1,0:T(2,128)(2,1)S(1)}, u32[]{:S(2)}, u32[]{:S(2)}) %all-to-all-start.2) | async-done | bytes 24608 | tf_op jit(solution)/shard_map/all_to_all | solution.py:19
  59.3 3.3 %all-to-all-start.3 = ((bf16[4,2,6144]{2,1,0:T(2,128)(2,1)}), bf16[4,2,6144]{2,1,0:T(2,128)(2,1)S(1)}, u32[]{:S(2)}, u32[]{:S(2)}) async-start(bf16[4,2,6144]{2,1,0:T(2,128)(2,1)} %reshape.86), calls=%async_computation.3 | async-start | bytes 196608 | tf_op jit(solution)/shard_map/all_to_all | solution.py:19
  63.3 4.0 %all-to-all-done.3 = bf16[4,2,6144]{2,1,0:T(2,128)(2,1)S(1)} async-done(((bf16[4,2,6144]{2,1,0:T(2,128)(2,1)}), bf16[4,2,6144]{2,1,0:T(2,128)(2,1)S(1)}, u32[]{:S(2)}, u32[]{:S(2)}) %all-to-all-start.3) | async-done | bytes 98336 | tf_op jit(solution)/shard_map/all_to_all | solution.py:19
  69.8 3.3 %fusion.27 = f32[1536,32]{0,1:T(8,128)S(1)} fusion(bf16[1,1536,1536]{2,1,0:T(8,128)(2,1)} %param.11, f32[1536,32]{0,1:T(8,128)S(1)} %fusion.6, pred[]{:T(512)S(6)} %eq.19), kind=kOutput, calls=%fused_computation.17 | convolution fusion | flops 151191552 | bytes 5111809 | tf_op jit(solution)/shard_map/dot_general | solution.py:96
  78.3 7.5 %all_to_all.71 = f32[4,1,12288]{2,1,0:T(1,128)S(1)} all-to-all(f32[4,1,12288]{2,1,0:T(1,128)S(1)} %reshape.88), channel_id=1, replica_groups=mesh['tc_0'=8,'tc_1'=4,'tc_2'=4,'pr'=2] {'tc_2'}, dimensions={0} | all-to-all | bytes 393216 | tf_op jit(solution)/shard_map/all_to_all | solution.py:44
  87.6 12.9 %all_to_all.72 = f32[32,1,384]{2,1,0:T(1,128)S(1)} all-to-all(f32[32,1,384]{2,1,0:T(1,128)S(1)} %reshape.90), channel_id=1, replica_groups=mesh['tc_0'=8,'tc_1'=4,'tc_2'=4,'pr'=2] {'tc_0','tc_1'}, dimensions={0} | all-to-all | bytes 98304 | tf_op jit(solution)/shard_map/all_to_all | solution.py:51
  102.2 3.9 %all-to-all-start.6 = ((bf16[32,2,192]{2,1,0:T(2,128)(2,1)}), bf16[32,2,192]{2,1,0:T(2,128)(2,1)S(1)}, u32[]{:S(2)}, u32[]{:S(2)}) async-start(bf16[32,2,192]{2,1,0:T(2,128)(2,1)} %reshape.92), calls=%async_computation.6 | async-start | bytes 65536 | tf_op jit(solution)/shard_map/all_to_all | solution.py:19
  107.2 7.4 %all-to-all-done.6 = bf16[32,2,192]{2,1,0:T(2,128)(2,1)S(1)} async-done(((bf16[32,2,192]{2,1,0:T(2,128)(2,1)}), bf16[32,2,192]{2,1,0:T(2,128)(2,1)S(1)}, u32[]{:S(2)}, u32[]{:S(2)}) %all-to-all-start.6) | async-done | bytes 24608 | tf_op jit(solution)/shard_map/all_to_all | solution.py:19
  116.0 3.5 %all-to-all-start.7 = ((bf16[4,2,6144]{2,1,0:T(2,128)(2,1)}), bf16[4,2,6144]{2,1,0:T(2,128)(2,1)S(1)}, u32[]{:S(2)}, u32[]{:S(2)}) async-start(bf16[4,2,6144]{2,1,0:T(2,128)(2,1)} %reshape.94), calls=%async_computation.7 | async-start | bytes 196608 | tf_op jit(solution)/shard_map/all_to_all | solution.py:19
  120.1 3.8 %all-to-all-done.7 = bf16[4,2,6144]{2,1,0:T(2,128)(2,1)S(1)} async-done(((bf16[4,2,6144]{2,1,0:T(2,128)(2,1)}), bf16[4,2,6144]{2,1,0:T(2,128)(2,1)S(1)}, u32[]{:S(2)}, u32[]{:S(2)}) %all-to-all-start.7) | async-done | bytes 98336 | tf_op jit(solution)/shard_map/all_to_all | solution.py:19
  127.1 3.3 %fusion.39 = f32[1536,32]{0,1:T(8,128)S(1)} fusion(bf16[1536,32]{0,1:T(8,128)(2,1)} %fusion.8, bf16[1,1536,1536]{2,1,0:T(8,128)(2,1)} %param.11, pred[]{:T(512)S(6)} %eq.15), kind=kOutput, calls=%fused_computation.21 | convolution fusion | flops 151142400 | bytes 5013505 | tf_op jit(solution)/shard_map/dot_general | solution.py:96
  133.8 2.6 %copy.111 = f32[4,32,12,32]{3,1,2,0:T(8,128)} copy(f32[4,32,12,32]{3,2,0,1:T(8,128)} %bitcast.124) | data formatting | bytes 393216 | tf_op jit(solution)/shard_map/transpose | solution.py:39
  137.9 7.5 %all_to_all.73 = f32[4,1,12288]{2,1,0:T(1,128)S(1)} all-to-all(f32[4,1,12288]{2,1,0:T(1,128)S(1)} %reshape.96), channel_id=1, replica_groups=mesh['tc_0'=8,'tc_1'=4,'tc_2'=4,'pr'=2] {'tc_2'}, dimensions={0} | all-to-all | bytes 393216 | tf_op jit(solution)/shard_map/all_to_all | solution.py:44
  149.2 11.7 %all_to_all.74 = f32[32,1,384]{2,1,0:T(1,128)S(1)} all-to-all(f32[32,1,384]{2,1,0:T(1,128)S(1)} %reshape.98), channel_id=1, replica_groups=mesh['tc_0'=8,'tc_1'=4,'tc_2'=4,'pr'=2] {'tc_0','tc_1'}, dimensions={0} | all-to-all | bytes 98304 | tf_op jit(solution)/shard_map/all_to_all | solution.py:51
  161.9 11.6 %all_to_all.75 = bf16[32,2,192]{2,1,0:T(2,128)(2,1)S(1)} all-to-all(bf16[32,2,192]{2,1,0:T(2,128)(2,1)S(1)} %reshape.100), channel_id=1, replica_groups=mesh['tc_0'=8,'tc_1'=4,'tc_2'=4,'pr'=2] {'tc_0','tc_1'}, dimensions={0} | all-to-all | bytes 49152 | tf_op jit(solution)/shard_map/all_to_all | solution.py:19
  174.8 3.3 %all-to-all-start.11 = ((bf16[4,2,6144]{2,1,0:T(2,128)(2,1)}), bf16[4,2,6144]{2,1,0:T(2,128)(2,1)S(1)}, u32[]{:S(2)}, u32[]{:S(2)}) async-start(bf16[4,2,6144]{2,1,0:T(2,128)(2,1)} %reshape.102), calls=%async_computation.11 | async-start | bytes 196608 | tf_op jit(solution)/shard_map/all_to_all | solution.py:19
  178.8 4.2 %all-to-all-done.11 = bf16[4,2,6144]{2,1,0:T(2,128)(2,1)S(1)} async-done(((bf16[4,2,6144]{2,1,0:T(2,128)(2,1)}), bf16[4,2,6144]{2,1,0:T(2,128)(2,1)S(1)}, u32[]{:S(2)}, u32[]{:S(2)}) %all-to-all-start.11) | async-done | bytes 98336 | tf_op jit(solution)/shard_map/all_to_all | solution.py:19
  183.9 18.0 %all_to_all.76 = bf16[2,3,768,32]{2,3,1,0:T(8,128)(2,1)S(1)} all-to-all(bf16[2,3,768,32]{2,3,1,0:T(8,128)(2,1)S(1)} %pad_maximum_fusion.1), channel_id=1, replica_groups=mesh['tc_0'=8,'tc_1'=4,'tc_2'=4,'pr'=2] {'pr'}, dimensions={0} | all-to-all | bytes 589824 | tf_op jit(solution)/shard_map/all_to_all | solution.py:121
  202.8 4.5 %all_to_all.77 = f32[2,2,3,64,200]{4,3,2,1,0:T(8,128)S(1)} all-to-all(f32[2,2,3,64,200]{4,3,2,1,0:T(8,128)S(1)} %broadcast_in_dim.91), channel_id=1, replica_groups=mesh['tc_0'=8,'tc_1'=4,'tc_2'=4,'pr'=2] {'pr'}, dimensions={0} | all-to-all | bytes 1228800 | tf_op jit(solution)/shard_map/all_to_all | solution.py:19
  (108 shorter events, 45.6 us)
Async XLA Ops:
  0.6 206.7 %copy-start = (bf16[2,3,200,768]{3,2,1,0:T(8,128)(2,1)S(1)}, bf16[2,3,200,768]{3,2,1,0:T(8,128)(2,1)}, u32[]{:S(2)}) copy-start(bf16[2,3,200,768]{3,2,1,0:T(8,128)(2,1)} %param.17) | copy-start | bytes 5529604
  11.3 23.9 %copy-start.7 = (s32[3]{0:T(128)S(1)}, s32[3]{0:T(128)}, u32[]{:S(2)}) copy-start(s32[3]{0:T(128)} %param.12) | copy-start | bytes 40
  22.9 29.7 %copy-start.9 = (s32[1,2]{1,0:T(1,128)S(1)}, s32[1,2]{1,0:T(1,128)}, u32[]{:S(2)}) copy-start(s32[1,2]{1,0:T(1,128)} %param.15) | copy-start | bytes 28
  24.1 19.8 %all-to-all-start.1 = ((f32[32,1,384]{2,1,0:T(1,128)}), f32[32,1,384]{2,1,0:T(1,128)S(1)}, u32[]{:S(2)}, u32[]{:S(2)}) async-start(f32[32,1,384]{2,1,0:T(1,128)} %reshape.82), calls=%async_computation.1 | async-start | bytes 98304 | tf_op jit(solution)/shard_map/all_to_all | solution.py:51
  45.5 12.5 %all-to-all-start.2 = ((bf16[32,2,192]{2,1,0:T(2,128)(2,1)}), bf16[32,2,192]{2,1,0:T(2,128)(2,1)S(1)}, u32[]{:S(2)}, u32[]{:S(2)}) async-start(bf16[32,2,192]{2,1,0:T(2,128)(2,1)} %reshape.84), calls=%async_computation.2 | async-start | bytes 65536 | tf_op jit(solution)/shard_map/all_to_all | solution.py:19
  58.3 9.6 %copy-start.5 = (f32[1,1536,32]{1,2,0:T(8,128)S(1)}, f32[1,1536,32]{1,2,0:T(8,128)}, u32[]{:S(2)}) copy-start(f32[1,1536,32]{1,2,0:T(8,128)} %param.10) | copy-start | bytes 589828
  59.3 7.9 %all-to-all-start.3 = ((bf16[4,2,6144]{2,1,0:T(2,128)(2,1)}), bf16[4,2,6144]{2,1,0:T(2,128)(2,1)S(1)}, u32[]{:S(2)}, u32[]{:S(2)}) async-start(bf16[4,2,6144]{2,1,0:T(2,128)(2,1)} %reshape.86), calls=%async_computation.3 | async-start | bytes 196608 | tf_op jit(solution)/shard_map/all_to_all | solution.py:19
  69.8 3.3 %copy-start.2 = (f32[1536,32]{0,1:T(8,128)}, f32[1536,32]{0,1:T(8,128)S(1)}, u32[]{:S(2)}) copy-start(f32[1536,32]{0,1:T(8,128)S(1)} %fusion.6) | copy-start | bytes 589828
  102.2 12.5 %all-to-all-start.6 = ((bf16[32,2,192]{2,1,0:T(2,128)(2,1)}), bf16[32,2,192]{2,1,0:T(2,128)(2,1)S(1)}, u32[]{:S(2)}, u32[]{:S(2)}) async-start(bf16[32,2,192]{2,1,0:T(2,128)(2,1)} %reshape.92), calls=%async_computation.6 | async-start | bytes 65536 | tf_op jit(solution)/shard_map/all_to_all | solution.py:19
  114.9 9.6 %copy-start.3 = (f32[1536,32]{0,1:T(8,128)S(1)}, f32[1536,32]{0,1:T(8,128)}, u32[]{:S(2)}) copy-start(f32[1536,32]{0,1:T(8,128)} %copy-done.2) | copy-start | bytes 589828
  116.0 7.9 %all-to-all-start.7 = ((bf16[4,2,6144]{2,1,0:T(2,128)(2,1)}), bf16[4,2,6144]{2,1,0:T(2,128)(2,1)S(1)}, u32[]{:S(2)}, u32[]{:S(2)}) async-start(bf16[4,2,6144]{2,1,0:T(2,128)(2,1)} %reshape.94), calls=%async_computation.7 | async-start | bytes 196608 | tf_op jit(solution)/shard_map/all_to_all | solution.py:19
  174.8 8.2 %all-to-all-start.11 = ((bf16[4,2,6144]{2,1,0:T(2,128)(2,1)}), bf16[4,2,6144]{2,1,0:T(2,128)(2,1)S(1)}, u32[]{:S(2)}, u32[]{:S(2)}) async-start(bf16[4,2,6144]{2,1,0:T(2,128)(2,1)} %reshape.102), calls=%async_computation.11 | async-start | bytes 196608 | tf_op jit(solution)/shard_map/all_to_all | solution.py:19
  183.8 18.1 %copy-start.1 = (bf16[2,3,200,768]{3,2,1,0:T(8,128)(2,1)S(1)}, bf16[2,3,200,768]{3,2,1,0:T(8,128)(2,1)}, u32[]{:S(2)}) copy-start(bf16[2,3,200,768]{3,2,1,0:T(8,128)(2,1)} %param.16) | copy-start | bytes 5529604
  183.8 18.8 %copy-start.4 = (bf16[3,1536,32]{1,2,0:T(8,128)(2,1)}, bf16[3,1536,32]{1,2,0:T(8,128)(2,1)S(1)}, u32[]{:S(2)}) copy-start(bf16[3,1536,32]{1,2,0:T(8,128)(2,1)S(1)} %pad_maximum_fusion) | copy-start | bytes 884740
  202.7 4.7 %copy-start.6 = (f32[2,64,768]{2,1,0:T(8,128)S(1)}, f32[2,64,768]{2,1,0:T(8,128)}, u32[]{:S(2)}) copy-start(f32[2,64,768]{2,1,0:T(8,128)} %param.19) | copy-start | bytes 1179652
  202.7 4.7 %copy-start.8 = (s32[2,3]{1,0:T(2,128)S(1)}, s32[2,3]{1,0:T(2,128)}, u32[]{:S(2)}) copy-start(s32[2,3]{1,0:T(2,128)} %param.18) | copy-start | bytes 76
